TPU v7x, 32 devices: a whole 2x2x4 slice. The times are simulated.
32 devices in a mesh: groups: 2 (over y), rows: 4 (over z), tm: 4 (over x, core).
Axes of the slice: x: 2, y: 2, z: 4, core: 2. Of those that a mesh axis runs over, the one named last changes fastest.
Arguments:
- video: bfloat16 [2, 16, 8, 96, 128], P('groups', 'tm', 'rows'), parts along dimension 0, may hold values from -6 to 6
- gamma_first: float32 [96], replicated, may hold values from 0.25 to 1.75
- kernel_first: bfloat16 [96, 2592], replicated, may hold values from -0.125 to 0.125
- bias_first: float32 [96], replicated, may hold values from -3 to 3
- gamma_second: float32 [96], replicated, may hold values from 0.25 to 1.75
- kernel_second: bfloat16 [96, 2592], replicated, may hold values from -0.125 to 0.125
- bias_second: float32 [96], replicated, may hold values from -3 to 3
Outputs:
- encoded: bfloat16 [2, 16, 8, 96, 128], P('groups', 'tm', 'rows'), parts along dimension 0
There are 2 independent parts, one for each index of `groups`. A program takes and returns all parts, laid end to end along the dimension named above; an argument that names none is the same for every part. Nothing has to cross between parts.
All inputs are finite; a program needn't handle non-finite values.
Results may differ from a plain program's by a relative error of at most 0.0036.
Values may be sent and summed in bfloat16 or wider, within the bound.
A program may use at most 64 MiB of HBM per device.

v0:
```python
import jax
import jax.numpy as jnp
from jax import lax
from jax.experimental import pallas as pl
from jax.experimental.pallas import tpu as pltpu
from jax.sharding import PartitionSpec as P

MESH = pl.DeviceIdType.MESH
epsilon = 1e-06


def block_kernel(
    video, k_first, k_second, g_first, b_first, g_second, b_second, out,
    ext, st_a, st_b, w_a, w_b, by_a, by_b, sum_a, sum_b, vecs, small_0, small_1, small_2, small_3, local_sem, send_sem, recv_sem,
):
    frames, rows, chans, width = video.shape[1:]
    group = 9 * chans
    t = lax.axis_index("tm")
    r = lax.axis_index("rows")
    has_prev = t > 0
    has_next = t < lax.axis_size("tm") - 1
    has_up = r > 0
    has_down = r < lax.axis_size("rows") - 1

    def both(one, other):
        return jnp.logical_and(one, other)

    up, down, later = {"rows": r - 1}, {"rows": r + 1}, {"tm": t + 1}

    barrier = pltpu.get_barrier_semaphore()
    for cond, where in ((has_up, up), (has_down, down), (has_prev, {"tm": t - 1})):
        @pl.when(cond)
        def _():
            pl.semaphore_signal(barrier, inc=1, device_id=where, device_id_type=MESH)

    own_rows = slice(2, 2 + rows)
    above, below = slice(0, 2), slice(2 + rows, 4 + rows)
    own = pltpu.make_async_copy(video.at[0], ext.at[frames:, own_rows], local_sem.at[0])
    load_a = pltpu.make_async_copy(k_first, w_a, local_sem.at[1])
    load_b = pltpu.make_async_copy(k_second, w_b, local_sem.at[2])
    own.start()
    small = [
        pltpu.make_async_copy(src, dst, local_sem.at[3 + n])
        for n, (src, dst) in enumerate(
            ((g_first, small_0), (b_first, small_1), (g_second, small_2), (b_second, small_3))
        )
    ]
    for copy in small:
        copy.start()
    load_a.start()
    load_b.start()

    own.wait()
    pl.semaphore_wait(
        barrier, has_up.astype(jnp.int32) + has_down.astype(jnp.int32) + has_next.astype(jnp.int32)
    )

    order = list(range(frames))[::-1]

    def plan(slot, src, dst, where, sends, takes):
        copy = pltpu.make_async_remote_copy(
            src_ref=src, dst_ref=dst, send_sem=send_sem.at[slot], recv_sem=recv_sem.at[slot],
            device_id=where, device_id_type=MESH,
        )
        return copy, sends, takes

    beside, passed = {}, {}
    for f in range(frames):
        mine = ext.at[frames + f, own_rows]
        beside[f] = (
            plan(f, mine, ext.at[frames + f, below], up, has_up, has_down),
            plan(frames + f, mine, ext.at[frames + f, above], down, has_down, has_up),
        )
        passed[f] = (
            plan(2 * frames + f, ext.at[frames + f, below], ext.at[f, below], later,
                 both(has_next, has_down), both(has_prev, has_down)),
            plan(3 * frames + f, ext.at[frames + f, above], ext.at[f, above], later,
                 both(has_next, has_up), both(has_prev, has_up)),
        )
    onward = plan(4 * frames, ext.at[frames:, own_rows], ext.at[0:frames, own_rows], later, has_next, has_prev)

    def start(made):
        for copy, sends, _ in made:
            pl.when(sends)(copy.start)

    def taken(made):
        for copy, _, takes in made:
            pl.when(takes)(copy.wait_recv)

    def sent(made):
        for copy, sends, _ in made:
            pl.when(sends)(copy.wait_send)

    start(beside[order[0]])
    start([onward])
    for f in order[1:]:
        start(beside[f])

    @pl.when(jnp.logical_not(has_up))
    def _():
        ext[:, above] = jnp.zeros((2 * frames, 2, chans, width), jnp.bfloat16)

    @pl.when(jnp.logical_not(has_down))
    def _():
        ext[:, below] = jnp.zeros((2 * frames, 2, chans, width), jnp.bfloat16)

    @pl.when(jnp.logical_not(has_prev))
    def _():
        ext[0:frames] = jnp.zeros((frames, rows + 4, chans, width), jnp.bfloat16)

    for n, ref in enumerate((small_0, small_1, small_2, small_3)):
        small[n].wait()
        vecs[n] = jnp.broadcast_to(ref[...], (width, chans)).T

    lane = lax.broadcasted_iota(jnp.int32, (chans, width), 1)

    def act(values, gain):
        meansq = jnp.sum(values * values, axis=0, keepdims=True) * (1.0 / chans)
        half = values * lax.rsqrt(meansq + epsilon) * (gain * 0.5)
        return half + half * jnp.tanh(half)

    def place(stack, many, f, p, field):
        shifted = [
            jnp.where(lane == 0, 0.0, pltpu.roll(field, 1, 1)).astype(jnp.bfloat16),
            field.astype(jnp.bfloat16),
            jnp.where(lane == width - 1, 0.0, pltpu.roll(field, width - 1, 1)).astype(jnp.bfloat16),
        ]
        for row in range(many):
            j = p - row
            if 0 <= j < 3:
                for k in range(3):
                    at = f * group + (j * 3 + k) * chans
                    stack[at : at + chans, row * width : (row + 1) * width] = shifted[k]

    def first_at(f, places):
        for p in places:
            place(st_a, rows + 2, f, p, act(ext[f, p].astype(jnp.float32), vecs[0]))

    def split(weights, by_frame):
        for i in range(3):
            by_frame[i * chans : (i + 1) * chans, :] = weights[:, i * group : (i + 1) * group]

    def conv_step(by_frame, stack, sums, count, g):
        low, high = max(0, g - count + 1), min(2, g)
        total = jnp.dot(
            by_frame[low * chans : (high + 1) * chans, :], stack[g * group : (g + 1) * group, :],
            preferred_element_type=jnp.float32,
        )
        whole = None
        for i in range(low, high + 1):
            part = total[(i - low) * chans : (i - low + 1) * chans]
            if i == 2:
                sums[g - i] = part
            elif i == 1:
                sums[g - i] += part
            else:
                whole = sums[g] + part
        return whole

    one = jnp.float32(1.0)
    inside_up = jnp.where(has_up, one, 0.0)
    inside_down = jnp.where(has_down, one, 0.0)
    inside_prev = jnp.where(has_prev, one, 0.0)

    def step(g):
        total = conv_step(by_a, st_a, sum_a, frames + 2, g)
        if total is None:
            return
        for row in range(rows + 2):
            value = act(total[:, row * width : (row + 1) * width] + vecs[1], vecs[2])
            if row == 0:
                value = value * inside_up
            if row == rows + 1:
                value = value * inside_down
            if g < 2:
                value = value * inside_prev
            place(st_b, rows, g, row, value)
        total = conv_step(by_b, st_b, sum_b, frames, g)
        if total is None:
            return
        for row in range(rows):
            value = total[:, row * width : (row + 1) * width] + vecs[3]
            out[0, g, row] = (ext[frames + g, row + 2].astype(jnp.float32) + value).astype(jnp.bfloat16)

    middle = range(2, 2 + rows)
    edges = [0, 1, 2 + rows, 3 + rows]
    for f in order:
        first_at(frames + f, middle)
    load_a.wait()
    split(w_a, by_a)
    load_b.wait()
    split(w_b, by_b)
    for f in order:
        taken(beside[f])
        start(passed[f])
        first_at(frames + f, edges)
        step(frames + f)
    taken([onward])
    for f in order:
        first_at(f, middle)
    for f in order:
        taken(passed[f])
        first_at(f, edges)
        step(f)
    for f in order:
        sent(beside[f])
        sent(passed[f])
    sent([onward])


def local(video, gamma_first, kernel_first, bias_first, gamma_second, kernel_second, bias_second):
    frames, rows, chans, width = video.shape[1:]
    ext = pltpu.VMEM((2 * frames, rows + 4, chans, width), jnp.bfloat16)
    wide = pltpu.VMEM((2 * frames * 9 * chans, (rows + 2) * width), jnp.bfloat16)
    stack = pltpu.VMEM(((frames + 2) * 9 * chans, rows * width), jnp.bfloat16)
    weights = pltpu.VMEM(kernel_first.shape, jnp.bfloat16)
    by_frame = pltpu.VMEM((3 * chans, 9 * chans), jnp.bfloat16)
    vmem = pl.BlockSpec(memory_space=pltpu.VMEM)
    hbm = pl.BlockSpec(memory_space=pl.ANY)
    return pl.pallas_call(
        block_kernel,
        out_shape=pltpu.VMEM(video.shape, jnp.bfloat16),
        in_specs=[hbm] * 7,
        out_specs=vmem,
        scratch_shapes=[
            ext, wide, stack, weights, weights, by_frame, by_frame,
            pltpu.VMEM((frames + 2, chans, (rows + 2) * width), jnp.float32),
            pltpu.VMEM((frames, chans, rows * width), jnp.float32),
            pltpu.VMEM((4, chans, width), jnp.float32),
            *[pltpu.VMEM((1, chans), jnp.float32)] * 4,
            pltpu.SemaphoreType.DMA((7,)),
            pltpu.SemaphoreType.DMA((4 * frames + 1,)),
            pltpu.SemaphoreType.DMA((4 * frames + 1,)),
        ],
        compiler_params=pltpu.CompilerParams(collective_id=0, has_side_effects=True),
        name="residual_block",
    )(
        video, kernel_first, kernel_second, gamma_first[None, :], bias_first[None, :],
        gamma_second[None, :], bias_second[None, :],
    )


def solution(mesh):
    in_specs = (P("groups", "tm", "rows", None, None), P(), P(), P(), P(), P(), P())
    out_specs = P("groups", "tm", "rows", None, None)
    return jax.shard_map(local, mesh=mesh, in_specs=in_specs, out_specs=out_specs, check_vma=False)
```

profile of v0, /device:TPU:0, one launch (start us, length us, event | category | flops | bytes accessed | tf_op | source)
XLA Modules:
  0.0 16.5 jit_solution(5425066835218427514)
XLA Ops:
  0.0 15.8 %residual_block.1 = bf16[1,4,2,96,128]{4,3,2,1,0:T(8,128)(2,1)S(1)} custom-call(bf16[1,4,2,96,128]{4,3,2,1,0:T(8,128)(2,1)} %video.1, bf16[96,2592]{1,0:T(8,128)(2,1)} %k_first.1, bf16[96,2592]{1,0:T(8,128)(2,1)} %k_second.1, f32[1,96]{1,0:T(1,128)} %bitcast.4, f32[1,96]{1,0:T(1,128)} %bitcast.5, f32[1,96]{1,0:T(1,128)} %bitcast.6, f32[1,96]{1,0:T(1,128)} %bitcast.7), custom_call_target="tpu_custom_call" | custom-call | tf_op jit(solution)/shard_map/residual_block/pallas_call | solution.py:220
  15.9 0.7 %copy.9 = bf16[1,4,2,96,128]{4,3,2,1,0:T(8,128)(2,1)} copy(bf16[1,4,2,96,128]{4,3,2,1,0:T(8,128)(2,1)S(1)} %residual_block.1) | data formatting | bytes 393216
where the time goes:
time: 16.7 us; the launch traced here: 16.5 us
  Pallas kernels  15.8 us (95%)
  local copies, waits for them, and re-layouts  0.68 us (4%)
    pallas_call x1, Pallas kernels, local(): pl.pallas_call(block_kernel, out_shape=pltpu.VMEM(video.shape, jnp.bfloat...  15.8 us
    unnamed x1, local copies, waits for them, and re-layouts  0.68 us

commit v1 on v0

--- a/solution.py
+++ b/solution.py
@@ -104,10 +104,6 @@
     def _():
         ext[:, below] = jnp.zeros((2 * frames, 2, chans, width), jnp.bfloat16)
 
-    @pl.when(jnp.logical_not(has_prev))
-    def _():
-        ext[0:frames] = jnp.zeros((frames, rows + 4, chans, width), jnp.bfloat16)
-
     for n, ref in enumerate((small_0, small_1, small_2, small_3)):
         small[n].wait()
         vecs[n] = jnp.broadcast_to(ref[...], (width, chans)).T
@@ -119,68 +115,89 @@
         half = values * lax.rsqrt(meansq + epsilon) * (gain * 0.5)
         return half + half * jnp.tanh(half)
 
-    def place(stack, many, f, p, field):
+    def place(stack, f, p, field):
         shifted = [
             jnp.where(lane == 0, 0.0, pltpu.roll(field, 1, 1)).astype(jnp.bfloat16),
             field.astype(jnp.bfloat16),
             jnp.where(lane == width - 1, 0.0, pltpu.roll(field, width - 1, 1)).astype(jnp.bfloat16),
         ]
-        for row in range(many):
-            j = p - row
-            if 0 <= j < 3:
-                for k in range(3):
-                    at = f * group + (j * 3 + k) * chans
-                    stack[at : at + chans, row * width : (row + 1) * width] = shifted[k]
+        for k in range(3):
+            at = (p * 3 + k) * chans
+            stack[f, at : at + chans, :] = shifted[k]
 
     def first_at(f, places):
         for p in places:
-            place(st_a, rows + 2, f, p, act(ext[f, p].astype(jnp.float32), vecs[0]))
+            place(st_a, f, p, act(ext[f, p].astype(jnp.float32), vecs[0]))
 
     def split(weights, by_frame):
         for i in range(3):
             by_frame[i * chans : (i + 1) * chans, :] = weights[:, i * group : (i + 1) * group]
 
-    def conv_step(by_frame, stack, sums, count, g):
-        low, high = max(0, g - count + 1), min(2, g)
+    def windows(stack, f, many):
+        return jnp.concatenate(
+            [stack[f, p * 3 * chans : (p + 3) * 3 * chans, :] for p in range(many)], axis=1
+        )
+
+    def taps(by_frame, stack, many, count, f):
+        low, high = max(0, f - count + 1), min(2, f)
         total = jnp.dot(
-            by_frame[low * chans : (high + 1) * chans, :], stack[g * group : (g + 1) * group, :],
+            by_frame[low * chans : (high + 1) * chans, :], windows(stack, f, many),
             preferred_element_type=jnp.float32,
         )
-        whole = None
-        for i in range(low, high + 1):
-            part = total[(i - low) * chans : (i - low + 1) * chans]
-            if i == 2:
-                sums[g - i] = part
-            elif i == 1:
-                sums[g - i] += part
-            else:
-                whole = sums[g] + part
-        return whole
+        return {f - i: total[(i - low) * chans : (i - low + 1) * chans] for i in range(low, high + 1)}
 
     one = jnp.float32(1.0)
     inside_up = jnp.where(has_up, one, 0.0)
     inside_down = jnp.where(has_down, one, 0.0)
-    inside_prev = jnp.where(has_prev, one, 0.0)
-
-    def step(g):
-        total = conv_step(by_a, st_a, sum_a, frames + 2, g)
-        if total is None:
-            return
-        for row in range(rows + 2):
-            value = act(total[:, row * width : (row + 1) * width] + vecs[1], vecs[2])
-            if row == 0:
-                value = value * inside_up
-            if row == rows + 1:
-                value = value * inside_down
-            if g < 2:
-                value = value * inside_prev
-            place(st_b, rows, g, row, value)
-        total = conv_step(by_b, st_b, sum_b, frames, g)
-        if total is None:
-            return
-        for row in range(rows):
-            value = total[:, row * width : (row + 1) * width] + vecs[3]
-            out[0, g, row] = (ext[frames + g, row + 2].astype(jnp.float32) + value).astype(jnp.bfloat16)
+
+    class Path:
+        def __init__(self, earlier):
+            self.first_left = {
+                o: {f for f in range(o, o + 3) if earlier or f >= frames} for o in range(frames + 2)
+            }
+            self.second_left = {
+                o: {f for f in range(o, o + 3) if earlier or f >= 2} for o in range(frames)
+            }
+            self.begun, self.ready = set(), []
+
+        def first_conv(self, f):
+            for o, part in taps(by_a, st_a, rows + 2, frames + 2, f).items():
+                if ("a", o) in self.begun:
+                    sum_a[o] += part
+                else:
+                    sum_a[o] = part
+                    self.begun.add(("a", o))
+                self.first_left[o].discard(f)
+                if not self.first_left[o]:
+                    self.ready.append(o)
+
+        def second_act(self, o):
+            for row in range(rows + 2):
+                value = act(sum_a[o, :, row * width : (row + 1) * width] + vecs[1], vecs[2])
+                if row == 0:
+                    value = value * inside_up
+                if row == rows + 1:
+                    value = value * inside_down
+                place(st_b, o, row, value)
+
+        def second_conv(self, f):
+            for o, part in taps(by_b, st_b, rows, frames, f).items():
+                if ("b", o) in self.begun:
+                    part = sum_b[o] + part
+                self.begun.add(("b", o))
+                self.second_left[o].discard(f)
+                if self.second_left[o]:
+                    sum_b[o] = part
+                    continue
+                for row in range(rows):
+                    value = part[:, row * width : (row + 1) * width] + vecs[3]
+                    out[0, o, row] = (ext[frames + o, row + 2].astype(jnp.float32) + value).astype(jnp.bfloat16)
+
+        def finish(self):
+            ready, self.ready = self.ready, []
+            for o in ready:
+                self.second_act(o)
+                self.second_conv(o)
 
     middle = range(2, 2 + rows)
     edges = [0, 1, 2 + rows, 3 + rows]
@@ -190,18 +207,45 @@
     split(w_a, by_a)
     load_b.wait()
     split(w_b, by_b)
-    for f in order:
+
+    def own_frame(path, f, extra=()):
         taken(beside[f])
         start(passed[f])
         first_at(frames + f, edges)
-        step(frames + f)
-    taken([onward])
-    for f in order:
-        first_at(f, middle)
-    for f in order:
+        for e in extra:
+            first_at(e, middle)
+        ready, path.ready = path.ready, []
+        path.first_conv(frames + f)
+        for o in ready:
+            path.second_act(o)
+            path.second_conv(o)
+
+    def earlier_frame(path, f):
         taken(passed[f])
         first_at(f, edges)
-        step(f)
+        ready, path.ready = path.ready, []
+        path.first_conv(f)
+        for o in ready:
+            path.second_act(o)
+            path.second_conv(o)
+
+    @pl.when(jnp.logical_not(has_prev))
+    def _():
+        path = Path(False)
+        for f in order:
+            own_frame(path, f)
+        path.finish()
+
+    @pl.when(has_prev)
+    def _():
+        path = Path(True)
+        onward[0].wait_recv()
+        for f in order:
+            own_frame(path, f, (f,))
+        for f in order:
+            earlier_frame(path, f)
+        path.finish()
+
     for f in order:
         sent(beside[f])
         sent(passed[f])
@@ -211,8 +255,8 @@
 def local(video, gamma_first, kernel_first, bias_first, gamma_second, kernel_second, bias_second):
     frames, rows, chans, width = video.shape[1:]
     ext = pltpu.VMEM((2 * frames, rows + 4, chans, width), jnp.bfloat16)
-    wide = pltpu.VMEM((2 * frames * 9 * chans, (rows + 2) * width), jnp.bfloat16)
-    stack = pltpu.VMEM(((frames + 2) * 9 * chans, rows * width), jnp.bfloat16)
+    wide = pltpu.VMEM((2 * frames, (rows + 4) * 3 * chans, width), jnp.bfloat16)
+    stack = pltpu.VMEM((frames + 2, (rows + 2) * 3 * chans, width), jnp.bfloat16)
     weights = pltpu.VMEM(kernel_first.shape, jnp.bfloat16)
     by_frame = pltpu.VMEM((3 * chans, 9 * chans), jnp.bfloat16)
     vmem = pl.BlockSpec(memory_space=pltpu.VMEM)

time: 16.7 us -> 14 us (0.84)
  the two profiles are of different devices: /device:TPU:0 before, /device:TPU:1 now
where the time goes in v1:
time: 14 us; the launch traced here: 13.9 us
  Pallas kernels  13.2 us (94%)
  local copies, waits for them, and re-layouts  0.68 us (5%)
    pallas_call x1, Pallas kernels, local(): pl.pallas_call(block_kernel, out_shape=pltpu.VMEM(video.shape, jnp.bfloat...  13.2 us
    unnamed x1, local copies, waits for them, and re-layouts  0.68 us

profile of v1, /device:TPU:1, one launch (start us, length us, event | category | flops | bytes accessed | tf_op | source)
XLA Modules:
  0.0 13.9 jit_solution(5918986324358509185)
XLA Ops:
  0.0 13.2 %residual_block.1 = bf16[1,4,2,96,128]{4,3,2,1,0:T(8,128)(2,1)S(1)} custom-call(bf16[1,4,2,96,128]{4,3,2,1,0:T(8,128)(2,1)} %video.1, bf16[96,2592]{1,0:T(8,128)(2,1)} %k_first.1, bf16[96,2592]{1,0:T(8,128)(2,1)} %k_second.1, f32[1,96]{1,0:T(1,128)} %bitcast.4, f32[1,96]{1,0:T(1,128)} %bitcast.5, f32[1,96]{1,0:T(1,128)} %bitcast.6, f32[1,96]{1,0:T(1,128)} %bitcast.7), custom_call_target="tpu_custom_call" | custom-call | tf_op jit(solution)/shard_map/residual_block/pallas_call | solution.py:264
  13.2 0.7 %copy.9 = bf16[1,4,2,96,128]{4,3,2,1,0:T(8,128)(2,1)} copy(bf16[1,4,2,96,128]{4,3,2,1,0:T(8,128)(2,1)S(1)} %residual_block.1) | data formatting | bytes 393216

commit v2 on v1

--- a/solution.py
+++ b/solution.py
@@ -106,13 +106,14 @@
 
     for n, ref in enumerate((small_0, small_1, small_2, small_3)):
         small[n].wait()
-        vecs[n] = jnp.broadcast_to(ref[...], (width, chans)).T
+        vecs[n] = jnp.broadcast_to(ref[...] * (0.5 if n % 2 == 0 else 1.0), (width, chans)).T
 
     lane = lax.broadcasted_iota(jnp.int32, (chans, width), 1)
 
-    def act(values, gain):
+    def act(values, half_gain, keep=None):
         meansq = jnp.sum(values * values, axis=0, keepdims=True) * (1.0 / chans)
-        half = values * lax.rsqrt(meansq + epsilon) * (gain * 0.5)
+        factor = lax.rsqrt(meansq + epsilon)
+        half = values * (factor if keep is None else factor * keep) * half_gain
         return half + half * jnp.tanh(half)
 
     def place(stack, f, p, field):
@@ -133,17 +134,18 @@
         for i in range(3):
             by_frame[i * chans : (i + 1) * chans, :] = weights[:, i * group : (i + 1) * group]
 
-    def windows(stack, f, many):
-        return jnp.concatenate(
-            [stack[f, p * 3 * chans : (p + 3) * 3 * chans, :] for p in range(many)], axis=1
-        )
-
-    def taps(by_frame, stack, many, count, f):
+    def taps(by_frame, stack, many, count, f, pieces):
         low, high = max(0, f - count + 1), min(2, f)
-        total = jnp.dot(
-            by_frame[low * chans : (high + 1) * chans, :], windows(stack, f, many),
-            preferred_element_type=jnp.float32,
-        )
+        total = None
+        for begin, end in pieces:
+            window = jnp.concatenate(
+                [stack[f, p * 3 * chans + begin : p * 3 * chans + end, :] for p in range(many)], axis=1
+            )
+            part = jnp.dot(
+                by_frame[low * chans : (high + 1) * chans, begin:end], window,
+                preferred_element_type=jnp.float32,
+            )
+            total = part if total is None else total + part
         return {f - i: total[(i - low) * chans : (i - low + 1) * chans] for i in range(low, high + 1)}
 
     one = jnp.float32(1.0)
@@ -158,10 +160,10 @@
             self.second_left = {
                 o: {f for f in range(o, o + 3) if earlier or f >= 2} for o in range(frames)
             }
-            self.begun, self.ready = set(), []
+            self.begun, self.multiply, self.ready, self.placed = set(), [], [], []
 
         def first_conv(self, f):
-            for o, part in taps(by_a, st_a, rows + 2, frames + 2, f).items():
+            for o, part in taps(by_a, st_a, rows + 2, frames + 2, f, ((0, group),)).items():
                 if ("a", o) in self.begun:
                     sum_a[o] += part
                 else:
@@ -173,15 +175,12 @@
 
         def second_act(self, o):
             for row in range(rows + 2):
-                value = act(sum_a[o, :, row * width : (row + 1) * width] + vecs[1], vecs[2])
-                if row == 0:
-                    value = value * inside_up
-                if row == rows + 1:
-                    value = value * inside_down
+                keep = {0: inside_up, rows + 1: inside_down}.get(row)
+                value = act(sum_a[o, :, row * width : (row + 1) * width] + vecs[1], vecs[2], keep)
                 place(st_b, o, row, value)
 
         def second_conv(self, f):
-            for o, part in taps(by_b, st_b, rows, frames, f).items():
+            for o, part in taps(by_b, st_b, rows, frames, f, ((0, 512), (512, group))).items():
                 if ("b", o) in self.begun:
                     part = sum_b[o] + part
                 self.begun.add(("b", o))
@@ -193,11 +192,29 @@
                     value = part[:, row * width : (row + 1) * width] + vecs[3]
                     out[0, o, row] = (ext[frames + o, row + 2].astype(jnp.float32) + value).astype(jnp.bfloat16)
 
-        def finish(self):
+        def advance(self, arrived=(), extra=(), now=False):
+            multiply, self.multiply = self.multiply, []
             ready, self.ready = self.ready, []
+            placed, self.placed = self.placed, []
+            for f in multiply:
+                self.first_conv(f)
+            for o in placed:
+                self.second_conv(o)
+            for f in arrived:
+                first_at(f, edges)
+                if now:
+                    self.first_conv(f)
+                else:
+                    self.multiply.append(f)
             for o in ready:
                 self.second_act(o)
-                self.second_conv(o)
+                self.placed.append(o)
+            for f in extra:
+                first_at(f, middle)
+
+        def finish(self):
+            while self.multiply or self.ready or self.placed:
+                self.advance()
 
     middle = range(2, 2 + rows)
     edges = [0, 1, 2 + rows, 3 + rows]
@@ -208,26 +225,14 @@
     load_b.wait()
     split(w_b, by_b)
 
-    def own_frame(path, f, extra=()):
+    def own_frame(path, f, extra=(), now=True):
         taken(beside[f])
         start(passed[f])
-        first_at(frames + f, edges)
-        for e in extra:
-            first_at(e, middle)
-        ready, path.ready = path.ready, []
-        path.first_conv(frames + f)
-        for o in ready:
-            path.second_act(o)
-            path.second_conv(o)
-
-    def earlier_frame(path, f):
+        path.advance((frames + f,), extra, now)
+
+    def earlier_frame(path, f, now=True):
         taken(passed[f])
-        first_at(f, edges)
-        ready, path.ready = path.ready, []
-        path.first_conv(f)
-        for o in ready:
-            path.second_act(o)
-            path.second_conv(o)
+        path.advance((f,), (), now)
 
     @pl.when(jnp.logical_not(has_prev))
     def _():
@@ -241,9 +246,9 @@
         path = Path(True)
         onward[0].wait_recv()
         for f in order:
-            own_frame(path, f, (f,))
+            own_frame(path, f, (f,), f > 0)
         for f in order:
-            earlier_frame(path, f)
+            earlier_frame(path, f, f < 2)
         path.finish()
 
     for f in order:

time: 14 us -> 13.3 us (0.950)
  Pallas kernels: 13.2 us -> 12.4 us
    pallas_call x1, Pallas kernels: 13.2 us -> 12.4 us  [local(): pl.pallas_call(block_kernel, out_shape=pltpu.VMEM(video.shape, jnp.bfloat...]
where the time goes in v2:
time: 13.3 us; the launch traced here: 13.1 us
  Pallas kernels  12.4 us (93%)
  local copies, waits for them, and re-layouts  0.68 us (5%)
    pallas_call x1, Pallas kernels, local(): pl.pallas_call(block_kernel, out_shape=pltpu.VMEM(video.shape, jnp.bfloat...  12.4 us
    unnamed x1, local copies, waits for them, and re-layouts  0.68 us

profile of v2, /device:TPU:1, one launch (start us, length us, event | category | flops | bytes accessed | tf_op | source)
XLA Modules:
  0.0 13.1 jit_solution(11841970205123542821)
XLA Ops:
  0.0 12.4 %residual_block.1 = bf16[1,4,2,96,128]{4,3,2,1,0:T(8,128)(2,1)S(1)} custom-call(bf16[1,4,2,96,128]{4,3,2,1,0:T(8,128)(2,1)} %video.1, bf16[96,2592]{1,0:T(8,128)(2,1)} %k_first.1, bf16[96,2592]{1,0:T(8,128)(2,1)} %k_second.1, f32[1,96]{1,0:T(1,128)} %bitcast.4, f32[1,96]{1,0:T(1,128)} %bitcast.5, f32[1,96]{1,0:T(1,128)} %bitcast.6, f32[1,96]{1,0:T(1,128)} %bitcast.7), custom_call_target="tpu_custom_call" | custom-call | tf_op jit(solution)/shard_map/residual_block/pallas_call | solution.py:269
  12.4 0.7 %copy.9 = bf16[1,4,2,96,128]{4,3,2,1,0:T(8,128)(2,1)} copy(bf16[1,4,2,96,128]{4,3,2,1,0:T(8,128)(2,1)S(1)} %residual_block.1) | data formatting | bytes 393216

commit v3 on v2

--- a/solution.py
+++ b/solution.py
@@ -22,9 +22,6 @@
     has_up = r > 0
     has_down = r < lax.axis_size("rows") - 1
 
-    def both(one, other):
-        return jnp.logical_and(one, other)
-
     up, down, later = {"rows": r - 1}, {"rows": r + 1}, {"tm": t + 1}
 
     barrier = pltpu.get_barrier_semaphore()
@@ -33,8 +30,8 @@
         def _():
             pl.semaphore_signal(barrier, inc=1, device_id=where, device_id_type=MESH)
 
-    own_rows = slice(2, 2 + rows)
-    above, below = slice(0, 2), slice(2 + rows, 4 + rows)
+    above, below, around, own_rows = slice(0, 2), slice(2, 4), slice(0, 4), slice(4, 4 + rows)
+    held_at = [0, 1, *range(4, 4 + rows), 2, 3]
     own = pltpu.make_async_copy(video.at[0], ext.at[frames:, own_rows], local_sem.at[0])
     load_a = pltpu.make_async_copy(k_first, w_a, local_sem.at[1])
     load_b = pltpu.make_async_copy(k_second, w_b, local_sem.at[2])
@@ -47,8 +44,6 @@
     ]
     for copy in small:
         copy.start()
-    load_a.start()
-    load_b.start()
 
     own.wait()
     pl.semaphore_wait(
@@ -72,12 +67,9 @@
             plan(frames + f, mine, ext.at[frames + f, above], down, has_down, has_up),
         )
         passed[f] = (
-            plan(2 * frames + f, ext.at[frames + f, below], ext.at[f, below], later,
-                 both(has_next, has_down), both(has_prev, has_down)),
-            plan(3 * frames + f, ext.at[frames + f, above], ext.at[f, above], later,
-                 both(has_next, has_up), both(has_prev, has_up)),
-        )
-    onward = plan(4 * frames, ext.at[frames:, own_rows], ext.at[0:frames, own_rows], later, has_next, has_prev)
+            plan(2 * frames + f, ext.at[frames + f, around], ext.at[f, around], later, has_next, has_prev),
+        )
+    onward = plan(3 * frames, ext.at[frames:, own_rows], ext.at[0:frames, own_rows], later, has_next, has_prev)
 
     def start(made):
         for copy, sends, _ in made:
@@ -96,13 +88,16 @@
     for f in order[1:]:
         start(beside[f])
 
+    load_a.start()
+    load_b.start()
+
     @pl.when(jnp.logical_not(has_up))
     def _():
-        ext[:, above] = jnp.zeros((2 * frames, 2, chans, width), jnp.bfloat16)
+        ext[frames:, above] = jnp.zeros((frames, 2, chans, width), jnp.bfloat16)
 
     @pl.when(jnp.logical_not(has_down))
     def _():
-        ext[:, below] = jnp.zeros((2 * frames, 2, chans, width), jnp.bfloat16)
+        ext[frames:, below] = jnp.zeros((frames, 2, chans, width), jnp.bfloat16)
 
     for n, ref in enumerate((small_0, small_1, small_2, small_3)):
         small[n].wait()
@@ -128,7 +123,7 @@
 
     def first_at(f, places):
         for p in places:
-            place(st_a, f, p, act(ext[f, p].astype(jnp.float32), vecs[0]))
+            place(st_a, f, p, act(ext[f, held_at[p]].astype(jnp.float32), vecs[0]))
 
     def split(weights, by_frame):
         for i in range(3):
@@ -190,7 +185,7 @@
                     continue
                 for row in range(rows):
                     value = part[:, row * width : (row + 1) * width] + vecs[3]
-                    out[0, o, row] = (ext[frames + o, row + 2].astype(jnp.float32) + value).astype(jnp.bfloat16)
+                    out[0, o, row] = (ext[frames + o, held_at[row + 2]].astype(jnp.float32) + value).astype(jnp.bfloat16)
 
         def advance(self, arrived=(), extra=(), now=False):
             multiply, self.multiply = self.multiply, []
@@ -278,8 +273,8 @@
             pltpu.VMEM((4, chans, width), jnp.float32),
             *[pltpu.VMEM((1, chans), jnp.float32)] * 4,
             pltpu.SemaphoreType.DMA((7,)),
-            pltpu.SemaphoreType.DMA((4 * frames + 1,)),
-            pltpu.SemaphoreType.DMA((4 * frames + 1,)),
+            pltpu.SemaphoreType.DMA((3 * frames + 1,)),
+            pltpu.SemaphoreType.DMA((3 * frames + 1,)),
         ],
         compiler_params=pltpu.CompilerParams(collective_id=0, has_side_effects=True),
         name="residual_block",

time: 13.3 us -> 13.2 us (level)
  no operation moved by 1% of the time
where the time goes in v3:
time: 13.2 us; the launch traced here: 13.1 us
  Pallas kernels  12.4 us (94%)
  local copies, waits for them, and re-layouts  0.68 us (5%)
    pallas_call x1, Pallas kernels, local(): pl.pallas_call(block_kernel, out_shape=pltpu.VMEM(video.shape, jnp.bfloat...  12.4 us
    unnamed x1, local copies, waits for them, and re-layouts  0.68 us

profile of v3, /device:TPU:1, one launch (start us, length us, event | category | flops | bytes accessed | tf_op | source)
XLA Modules:
  0.0 13.1 jit_solution(5213062694400467484)
XLA Ops:
  0.0 12.4 %residual_block.1 = bf16[1,4,2,96,128]{4,3,2,1,0:T(8,128)(2,1)S(1)} custom-call(bf16[1,4,2,96,128]{4,3,2,1,0:T(8,128)(2,1)} %video.1, bf16[96,2592]{1,0:T(8,128)(2,1)} %k_first.1, bf16[96,2592]{1,0:T(8,128)(2,1)} %k_second.1, f32[1,96]{1,0:T(1,128)} %bitcast.4, f32[1,96]{1,0:T(1,128)} %bitcast.5, f32[1,96]{1,0:T(1,128)} %bitcast.6, f32[1,96]{1,0:T(1,128)} %bitcast.7), custom_call_target="tpu_custom_call" | custom-call | tf_op jit(solution)/shard_map/residual_block/pallas_call | solution.py:264
  12.4 0.7 %copy.9 = bf16[1,4,2,96,128]{4,3,2,1,0:T(8,128)(2,1)} copy(bf16[1,4,2,96,128]{4,3,2,1,0:T(8,128)(2,1)S(1)} %residual_block.1) | data formatting | bytes 393216
